TPU v7x, 32 devices: a whole 2x2x4 slice. The times are simulated.
32 devices in a mesh: dp: 8 (over z, y), seq: 4 (over x, core).
Axes of the slice: x: 2, y: 2, z: 4, core: 2. Of those that a mesh axis runs over, the one named last changes fastest.
Arguments:
- tokens: bfloat16 [16384, 1024], P(('dp', 'seq')), may hold values from -6 to 6
- doc_starts: int32 [8, 4], P('dp'), may hold values from 0 to 2047, as said below
- routes: int32 [16384, 1], P(('dp', 'seq')), may hold values from 0 to 63; in each aligned block of 512 rows (0 to 511, 512 to 1023, ...) at most 16 rows name the same one
- ln1_gain: bfloat16 [1024], P('seq'), may hold values from 0.5 to 1.5
- ln1_bias: bfloat16 [1024], P('seq'), may hold values from -4 to 4
- w_qkv: bfloat16 [1024, 3072], P('seq'), may hold values from -0.1875 to 0.1875
- w_proj: bfloat16 [1024, 1024], P('seq'), may hold values from -0.75 to 0.75
- ln2_gain: bfloat16 [1024], P('seq'), may hold values from 0.5 to 1.5
- ln2_bias: bfloat16 [1024], P('seq'), may hold values from -4 to 4
- w_router: bfloat16 [1024, 64], P('seq'), may hold values from -0.09375 to 0.09375
- w_expert_in: bfloat16 [64, 1024, 4096], P('dp', None, 'seq'), may hold values from -0.1875 to 0.1875
- w_expert_out: bfloat16 [64, 4096, 1024], P('dp', 'seq'), may hold values from -12 to 12
- out_grad: bfloat16 [16384, 1024], P(('dp', 'seq')), may hold values from -6 to 6
Outputs:
- output: bfloat16 [16384, 1024], P(('dp', 'seq'))
- input_grad: float32 [16384, 1024], P(('dp', 'seq'))
- ln1_gain_grad: float32 [1024], P('seq')
- ln1_bias_grad: float32 [1024], P('seq')
- w_qkv_grad: float32 [1024, 3072], P('seq')
- w_proj_grad: float32 [1024, 1024], P('seq')
- ln2_gain_grad: float32 [1024], P('seq')
- ln2_bias_grad: float32 [1024], P('seq')
- w_router_grad: float32 [1024, 64], P('seq')
- w_expert_in_grad: float32 [64, 1024, 4096], P('dp', None, 'seq')
- w_expert_out_grad: float32 [64, 4096, 1024], P('dp', 'seq')
Inputs may be any that keep to these rules, and one draw needn't show every extreme that they name: `doc_starts`: each row begins with 0 and rises strictly; entry j is where document j of sequence r begins. `routes`: among the 512 rows of one device (aligned blocks), no expert is named more than 16 times, a bound that some block reaches.
All inputs are finite; a program needn't handle non-finite values.
Results may differ from a plain program's by a relative error of at most 0.02.
Values may be sent and summed in bfloat16 or wider, within the bound.
A program may use at most 320 MiB of HBM per device.

v0:
```python
import jax
import jax.numpy as jnp
from jax import lax
from jax.sharding import PartitionSpec as P

H = 16
HD = 64
EXPERTS = 64
TOK_DEV = 512
EPS = 1e-05
NEG = -1e30


def normalize(values):
    center = values - jnp.mean(values, axis=-1, keepdims=True)
    inverse = lax.rsqrt(jnp.mean(center * center, axis=-1, keepdims=True) + EPS)
    return (center * inverse, inverse)


def norm_back(grad_norm, normed, inverse):
    first_mean = jnp.mean(grad_norm, axis=-1, keepdims=True)
    second_mean = jnp.mean(grad_norm * normed, axis=-1, keepdims=True)
    return inverse * (grad_norm - first_mean - normed * second_mean)


def collect_rows(rows_part, grads_part):
    return (
        lax.all_gather(rows_part, "seq", axis=1, tiled=True),
        lax.all_gather(grads_part, "seq", axis=1, tiled=True),
    )


def route_rows(rows_part, grads_part):
    return (
        lax.all_to_all(rows_part, "dp", split_axis=0, concat_axis=0, tiled=True),
        lax.all_to_all(grads_part, "dp", split_axis=0, concat_axis=0, tiled=True),
    )


def expert_work(rows_in, grads_in, first_weight, second_weight):
    pre_act = jnp.einsum(
        "abecd,edf->abecf", rows_in, first_weight, preferred_element_type=jnp.float32
    )
    hidden_exp, gelu_back = jax.vjp(jax.nn.gelu, pre_act)
    hidden_low = hidden_exp.astype(jnp.bfloat16)
    part_out = jnp.einsum(
        "abecf,efd->abecd", hidden_low, second_weight, preferred_element_type=jnp.float32
    )
    grad_hidden = jnp.einsum(
        "abecd,efd->abecf", grads_in, second_weight, preferred_element_type=jnp.float32
    )
    grad_pre = gelu_back(grad_hidden)[0].astype(jnp.bfloat16)
    first_grad = jnp.einsum(
        "abecd,abecf->edf", rows_in, grad_pre, preferred_element_type=jnp.float32
    )
    second_grad = jnp.einsum(
        "abecf,abecd->efd", hidden_low, grads_in, preferred_element_type=jnp.float32
    )
    part_dx = jnp.einsum(
        "abecf,edf->abecd", grad_pre, first_weight, preferred_element_type=jnp.float32
    )
    return (part_out, part_dx, first_grad, second_grad)


def per_device(
    tokens,
    doc_starts,
    routes,
    ln1_gain,
    ln1_bias,
    w_qkv,
    w_proj,
    ln2_gain,
    ln2_bias,
    w_router,
    w_expert_in,
    w_expert_out,
    out_grad,
):
    seq_count = lax.axis_size("seq")
    dp_count = lax.axis_size("dp")
    gathered_weights = (
        lax.all_gather(w_qkv, "seq", axis=0, tiled=True),
        lax.all_gather(w_proj, "seq", axis=0, tiled=True),
        lax.all_gather(w_router, "seq", axis=0, tiled=True),
        lax.all_gather(ln1_gain, "seq", axis=0, tiled=True),
        lax.all_gather(ln1_bias, "seq", axis=0, tiled=True),
        lax.all_gather(ln2_gain, "seq", axis=0, tiled=True),
        lax.all_gather(ln2_bias, "seq", axis=0, tiled=True),
    )
    qkv_weight = gathered_weights[0]
    proj_weight = gathered_weights[1]
    router_weight = gathered_weights[2]
    gain_one = gathered_weights[3].astype(jnp.float32)
    bias_one = gathered_weights[4].astype(jnp.float32)
    gain_two = gathered_weights[5].astype(jnp.float32)
    bias_two = gathered_weights[6].astype(jnp.float32)
    inputs = tokens.astype(jnp.float32)
    row_count = inputs.shape[0]
    width = inputs.shape[1]
    normed_one, inverse_one = normalize(inputs)
    hidden_one = (normed_one * gain_one + bias_one).astype(jnp.bfloat16)
    qkv_local = jnp.dot(hidden_one, qkv_weight, preferred_element_type=jnp.float32).astype(
        jnp.bfloat16
    )
    heads_here = H // seq_count
    head_width = heads_here * HD
    length = row_count * seq_count
    qkv_heads = lax.all_to_all(
        qkv_local.reshape(row_count, 3, seq_count, head_width),
        "seq",
        split_axis=2,
        concat_axis=0,
        tiled=True,
    )
    queries = qkv_heads[:, 0, 0].reshape(length, heads_here, HD)
    key_rows = qkv_heads[:, 1, 0].reshape(length, heads_here, HD)
    value_rows = qkv_heads[:, 2, 0].reshape(length, heads_here, HD)
    starts = doc_starts[0]
    positions = jnp.arange(length, dtype=jnp.int32)
    doc_first = jnp.max(
        jnp.where(starts[None, :] <= positions[:, None], starts[None, :], 0), axis=1
    )
    block_rows = min(512, length)
    block_count = length // block_rows
    factor = HD ** (-0.5)

    def block_scores(block_index):
        begin = block_index * block_rows
        query_block = lax.dynamic_slice_in_dim(queries, begin, block_rows, 0)
        first_block = lax.dynamic_slice_in_dim(doc_first, begin, block_rows, 0)
        query_pos = begin + jnp.arange(block_rows, dtype=jnp.int32)
        allowed = (positions[None, :] <= query_pos[:, None]) & (
            positions[None, :] >= first_block[:, None]
        )
        scores = (
            jnp.einsum("qhd,khd->hqk", query_block, key_rows, preferred_element_type=jnp.float32)
            * factor
        )
        return jnp.where(allowed[None], scores, NEG)

    def forward_block(block_index):
        scores = block_scores(block_index)
        row_top = jnp.max(scores, axis=-1, keepdims=True)
        weights = jnp.exp(scores - row_top)
        totals = jnp.sum(weights, axis=-1, keepdims=True)
        probs_low = (weights / totals).astype(jnp.bfloat16)
        attended = jnp.einsum(
            "hqk,khd->qhd", probs_low, value_rows, preferred_element_type=jnp.float32
        ).astype(jnp.bfloat16)
        return (attended, (row_top + jnp.log(totals))[:, :, 0])

    attended_all, log_totals = lax.map(forward_block, jnp.arange(block_count, dtype=jnp.int32))
    heads_out = attended_all.reshape(length, head_width)
    token_heads = lax.all_to_all(heads_out, "seq", split_axis=0, concat_axis=1, tiled=True)
    middle = inputs + jnp.dot(token_heads, proj_weight, preferred_element_type=jnp.float32)
    normed_two, inverse_two = normalize(middle)
    hidden_two = (normed_two * gain_two + bias_two).astype(jnp.bfloat16)
    logits = jnp.dot(hidden_two, router_weight, preferred_element_type=jnp.float32)
    logit_top = jnp.max(logits, axis=-1, keepdims=True)
    logit_exp = jnp.exp(logits - logit_top)
    probs = logit_exp / jnp.sum(logit_exp, axis=-1, keepdims=True)
    expert_ids = routes[:, 0]
    expert_range = jnp.arange(EXPERTS, dtype=jnp.int32)
    selector = expert_ids[:, None] == expert_range[None, :]
    selector_float = selector.astype(jnp.float32)
    gate = jnp.sum(probs * selector_float, axis=1)
    capacity = max(2, 2 * TOK_DEV // EXPERTS)
    onehot_int = selector.astype(jnp.int32)
    ranking = jnp.sum((jnp.cumsum(onehot_int, axis=0) - 1) * onehot_int, axis=1)
    slot_ids = expert_ids * capacity + ranking
    placement_map = (
        jnp.arange(EXPERTS * capacity, dtype=jnp.int32)[:, None] == slot_ids[None, :]
    ).astype(jnp.bfloat16)
    grad_out = out_grad.astype(jnp.float32)
    scaled_grad = (gate[:, None] * grad_out).astype(jnp.bfloat16)
    local_experts = EXPERTS // dp_count
    buffer_shape = (dp_count, 1, local_experts, capacity, width)
    send_rows = (
        jnp.dot(placement_map, hidden_two, preferred_element_type=jnp.float32)
        .astype(jnp.bfloat16)
        .reshape(buffer_shape)
    )
    send_grads = (
        jnp.dot(placement_map, scaled_grad, preferred_element_type=jnp.float32)
        .astype(jnp.bfloat16)
        .reshape(buffer_shape)
    )
    collected = collect_rows(send_rows, send_grads)
    arrived = route_rows(collected[0], collected[1])
    part_out, part_dx, expert_in_grad, expert_out_grad = expert_work(
        arrived[0], arrived[1], w_expert_in, w_expert_out
    )
    summed_rows = (
        lax.psum_scatter(
            part_out.astype(jnp.bfloat16), "seq", scatter_dimension=1, tiled=True
        ).astype(jnp.float32),
        lax.psum_scatter(
            part_dx.astype(jnp.bfloat16), "seq", scatter_dimension=1, tiled=True
        ).astype(jnp.float32),
    )
    rows_out = summed_rows[0]
    rows_dx = summed_rows[1]
    back_rows = (
        lax.all_to_all(
            rows_out.astype(jnp.bfloat16), "dp", split_axis=0, concat_axis=0, tiled=True
        ),
        lax.all_to_all(rows_dx.astype(jnp.bfloat16), "dp", split_axis=0, concat_axis=0, tiled=True),
    )
    flat_out = back_rows[0].reshape(EXPERTS * capacity, width)
    flat_dx = back_rows[1].reshape(EXPERTS * capacity, width)
    expert_out = jnp.einsum(
        "sr,sd->rd", placement_map, flat_out, preferred_element_type=jnp.float32
    )
    expert_dx = jnp.einsum("sr,sd->rd", placement_map, flat_dx, preferred_element_type=jnp.float32)
    output = (middle + gate[:, None] * expert_out).astype(jnp.bfloat16)
    grad_gate = jnp.sum(grad_out * expert_out, axis=1)
    grad_logits = probs * (selector_float - gate[:, None]) * grad_gate[:, None]
    router_grad = jnp.dot(
        hidden_two.astype(jnp.float32).T, grad_logits, precision=lax.Precision.HIGHEST
    )
    grad_two = expert_dx + jnp.dot(
        grad_logits, router_weight.astype(jnp.float32).T, precision=lax.Precision.HIGHEST
    )
    gain_two_grad = jnp.sum(grad_two * normed_two, axis=0)
    bias_two_grad = jnp.sum(grad_two, axis=0)
    grad_middle = grad_out + norm_back(grad_two * gain_two, normed_two, inverse_two)
    grad_branch = grad_middle.astype(jnp.bfloat16)
    proj_grad = jnp.dot(token_heads.T, grad_branch, preferred_element_type=jnp.float32)
    grad_heads_tok = jnp.dot(grad_branch, proj_weight.T, preferred_element_type=jnp.float32).astype(
        jnp.bfloat16
    )
    grad_heads = lax.all_to_all(grad_heads_tok, "seq", split_axis=1, concat_axis=0, tiled=True)
    grad_attended = grad_heads.reshape(length, heads_here, HD)

    def backward_block(carry, block_index):
        key_acc, value_acc = carry
        begin = block_index * block_rows
        query_block = lax.dynamic_slice_in_dim(queries, begin, block_rows, 0)
        grad_block = lax.dynamic_slice_in_dim(grad_attended, begin, block_rows, 0)
        scores = block_scores(block_index)
        probs_block = jnp.exp(scores - log_totals[block_index][:, :, None])
        grad_probs = jnp.einsum(
            "qhd,khd->hqk", grad_block, value_rows, preferred_element_type=jnp.float32
        )
        row_dot = jnp.sum(probs_block * grad_probs, axis=-1, keepdims=True)
        grad_scores = (probs_block * (grad_probs - row_dot)).astype(jnp.bfloat16)
        grad_query = (
            jnp.einsum("hqk,khd->qhd", grad_scores, key_rows, preferred_element_type=jnp.float32)
            * factor
        ).astype(jnp.bfloat16)
        key_acc = (
            key_acc
            + jnp.einsum(
                "hqk,qhd->khd", grad_scores, query_block, preferred_element_type=jnp.float32
            )
            * factor
        )
        value_acc = value_acc + jnp.einsum(
            "hqk,qhd->khd",
            probs_block.astype(jnp.bfloat16),
            grad_block,
            preferred_element_type=jnp.float32,
        )
        return ((key_acc, value_acc), grad_query)

    zero_rows = jnp.zeros((length, heads_here, HD), jnp.float32)
    carried, query_grad = lax.scan(
        backward_block, (zero_rows, zero_rows), jnp.arange(block_count, dtype=jnp.int32)
    )
    grad_qkv_heads = jnp.stack(
        [
            query_grad.reshape(length, head_width),
            carried[0].astype(jnp.bfloat16).reshape(length, head_width),
            carried[1].astype(jnp.bfloat16).reshape(length, head_width),
        ],
        axis=1,
    )[:, :, None, :]
    grad_qkv = lax.all_to_all(
        grad_qkv_heads, "seq", split_axis=0, concat_axis=2, tiled=True
    ).reshape(row_count, 3 * width)
    qkv_grad = jnp.dot(hidden_one.T, grad_qkv, preferred_element_type=jnp.float32)
    grad_one = jnp.dot(grad_qkv, qkv_weight.T, preferred_element_type=jnp.float32)
    gain_one_grad = jnp.sum(grad_one * normed_one, axis=0)
    bias_one_grad = jnp.sum(grad_one, axis=0)
    input_grad = grad_middle + norm_back(grad_one * gain_one, normed_one, inverse_one)
    summed = (
        lax.psum_scatter(
            qkv_grad.astype(jnp.bfloat16), "seq", scatter_dimension=0, tiled=True
        ).astype(jnp.float32),
        lax.psum_scatter(
            proj_grad.astype(jnp.bfloat16), "seq", scatter_dimension=0, tiled=True
        ).astype(jnp.float32),
        lax.psum_scatter(
            router_grad.astype(jnp.bfloat16), "seq", scatter_dimension=0, tiled=True
        ).astype(jnp.float32),
        lax.psum_scatter(
            gain_one_grad.astype(jnp.bfloat16), "seq", scatter_dimension=0, tiled=True
        ).astype(jnp.float32),
        lax.psum_scatter(
            bias_one_grad.astype(jnp.bfloat16), "seq", scatter_dimension=0, tiled=True
        ).astype(jnp.float32),
        lax.psum_scatter(
            gain_two_grad.astype(jnp.bfloat16), "seq", scatter_dimension=0, tiled=True
        ).astype(jnp.float32),
        lax.psum_scatter(
            bias_two_grad.astype(jnp.bfloat16), "seq", scatter_dimension=0, tiled=True
        ).astype(jnp.float32),
    )
    reduced = (
        lax.psum(summed[0].astype(jnp.bfloat16), "dp").astype(jnp.float32),
        lax.psum(summed[1].astype(jnp.bfloat16), "dp").astype(jnp.float32),
        lax.psum(summed[2].astype(jnp.bfloat16), "dp").astype(jnp.float32),
        lax.psum(summed[3].astype(jnp.bfloat16), "dp").astype(jnp.float32),
        lax.psum(summed[4].astype(jnp.bfloat16), "dp").astype(jnp.float32),
        lax.psum(summed[5].astype(jnp.bfloat16), "dp").astype(jnp.float32),
        lax.psum(summed[6].astype(jnp.bfloat16), "dp").astype(jnp.float32),
    )
    return (
        output,
        input_grad,
        reduced[3],
        reduced[4],
        reduced[0],
        reduced[1],
        reduced[5],
        reduced[6],
        reduced[2],
        expert_in_grad,
        expert_out_grad,
    )


def solution(mesh):
    in_specs = (
        P(("dp", "seq"), None),
        P("dp", None),
        P(("dp", "seq"), None),
        P("seq"),
        P("seq"),
        P("seq", None),
        P("seq", None),
        P("seq"),
        P("seq"),
        P("seq", None),
        P("dp", None, "seq"),
        P("dp", "seq", None),
        P(("dp", "seq"), None),
    )
    out_specs = (
        P(("dp", "seq"), None),
        P(("dp", "seq"), None),
        P("seq"),
        P("seq"),
        P("seq", None),
        P("seq", None),
        P("seq"),
        P("seq"),
        P("seq", None),
        P("dp", None, "seq"),
        P("dp", "seq", None),
    )
    return jax.shard_map(
        per_device, mesh=mesh, in_specs=in_specs, out_specs=out_specs, check_vma=False
    )
```

profile of v0, /device:TPU:0, one launch (start us, length us, event | category | flops | bytes accessed | tf_op | source)
XLA Modules:
  0.0 1636.1 jit_solution(8930138773344012550)
XLA Ops:
  9.2 6.0 all-gather.1
  24.0 34.7 %all-gather.9.cloned.1.call-done = bf16[1024,3072]{1,0:T(8,128)(2,1)} async-done(((bf16[256,3072]{1,0:T(8,128)(2,1)}), bf16[1024,3072]{1,0:T(8,128)(2,1)}) %all-gather.9.cloned.1.call-update) | async-done | bytes 6291472 | tf_op jit(solution)/shard_map/all_gather | solution.py:83
  58.7 8.3 convolution_convert_fusion.1
  79.4 47.3 %all-to-all-done = bf16[512,3,4,256]{3,0,1,2:T(8,128)(2,1)S(1)} async-done(((bf16[512,3,4,256]{3,0,1,2:T(8,128)(2,1)}), bf16[512,3,4,256]{3,0,1,2:T(8,128)(2,1)S(1)}, u32[]{:S(2)}, u32[]{:S(2)}) %all-to-all-start) | async-done | bytes 3145760 | tf_op jit(solution)/shard_map/all_to_all | solution.py:109
  131.9 67.1 %while.30 = (s32[]{:T(128)}, bf16[4,512,4,64]{1,3,2,0:T(8,128)(2,1)}, f32[4,4,512]{2,1,0:T(4,128)}, s32[4]{0:T(128)S(1)}, s32[2048]{0:T(1024)S(1)}, /*index=5*/b...) while((s32[]{:T(128)}, ...), condition=%wide.region_6.7_spmd.clone.clone, body=%wide.region_3.6_spmd.clone.clone.sunk | while | flops 1127348736 | bytes 57223368 | solution.py:153
  142.1 5.9 fusion.172
  158.9 5.9 fusion.172
  175.6 5.9 fusion.172
  192.4 5.9 fusion.172
  203.3 15.3 all-gather.3
  232.5 58.4 %all-gather.13.cloned.1.call-done = bf16[8,4,8,16,1024]{4,3,1,2,0:T(8,128)(2,1)} async-done(((bf16[8,1,8,16,1024]{4,3,1,2,0:T(8,128)(2,1)}), bf16[8,4,8,16,1024]{4,3,1,2,0:T(8,128)(2,1)}) %all-gather.13.cloned.1.call-update) | async-done | bytes 8388624 | tf_op jit(solution)/shard_map/all_gather | solution.py:28
  307.7 58.9 %all-gather.15.cloned.1.call-done = bf16[8,4,8,16,1024]{4,3,1,2,0:T(8,128)(2,1)} async-done(((bf16[8,1,8,16,1024]{4,3,1,2,0:T(8,128)(2,1)}), bf16[8,4,8,16,1024]{4,3,1,2,0:T(8,128)(2,1)}) %all-gather.15.cloned.1.call-update) | async-done | bytes 8388624 | tf_op jit(solution)/shard_map/all_gather | solution.py:29
  366.6 113.5 %all-to-all-done.2 = bf16[8,4,8,16,1024]{4,3,1,2,0:T(8,128)(2,1)} async-done(((bf16[8,4,8,16,1024]{4,3,1,2,0:T(8,128)(2,1)}), bf16[8,4,8,16,1024]{4,3,1,2,0:T(8,128)(2,1)}, u32[]{:S(2)}, u32[]{:S(2)}) %all-to-all-start.2) | async-done | bytes 8388640 | tf_op jit(solution)/shard_map/all_to_all | solution.py:35
  485.3 24.4 %fusion.62 = (bf16[8,4,8,16,1024]{4,3,1,0,2:T(8,128)(2,1)}, f32[8,8,4,16,1024]{4,3,2,1,0:T(8,128)}) fusion(bf16[8,1024,1024]{2,1,0:T(8,128)(2,1)} %param.27, bf16[8,4,8,16,1024]{4,3,1,2,0:T(8,128)(2,1)} %all-to-all-done.2), kind=kOutput, calls=%fused_computation.76 | convolution fusion | flops 8627683328 | bytes 50331648 | tf_op jit(solution)/shard_map/abecd,edf->abecf/dot_general | solution.py:41
  509.7 158.0 %all-to-all-done.4 = bf16[8,4,8,16,1024]{4,3,1,2,0:T(8,128)(2,1)} async-done(((bf16[8,4,8,16,1024]{4,3,1,2,0:T(8,128)(2,1)}), bf16[8,4,8,16,1024]{4,3,1,2,0:T(8,128)(2,1)}, u32[]{:S(2)}, u32[]{:S(2)}) %all-to-all-start.4) | async-done | bytes 8388640 | tf_op jit(solution)/shard_map/all_to_all | solution.py:36
  667.6 25.7 %fusion.50 = bf16[8,4,8,16,1024]{4,3,1,0,2:T(8,128)(2,1)} fusion(f32[8,8,4,16,1024]{4,3,2,1,0:T(8,128)} %get-tuple-element.341, bf16[8,1024,1024]{2,1,0:T(8,128)(2,1)} %param.28, bf16[8,4,8,16,1024]{4,3,1,2,0:T(8,128)(2,1)} %all-to-all-done.4), kind=kOutput, calls=%fused_computation.61 | convolution fusion | flops 8673820672 | bytes 50331648 | tf_op jit(solution)/shard_map/abecd,efd->abecf/dot_general | solution.py:49
  693.4 15.9 convert_bitcast_fusion
  709.3 18.1 %convert_bitcast_fusion.1 = bf16[8,4,8,16,1024]{4,3,1,0,2:T(8,128)(2,1)} fusion(bf16[8,4,8,16,1024]{4,3,1,0,2:T(8,128)(2,1)} %get-tuple-element.340, bf16[8,1024,1024]{2,1,0:T(8,128)(2,1)} %param.28), kind=kOutput, calls=%fused_computation.84 | convolution fusion | flops 8594128896 | bytes 33554432 | tf_op jit(solution)/shard_map/abecf,efd->abecd/dot_general | solution.py:46
  728.6 285.9 %all-reduce.15.cloned.1.call-done = (bf16[8,4,8,16,1024]{4,3,1,0,2:T(8,128)(2,1)}, bf16[8,4,8,16,1024]{4,3,1,0,2:T(8,128)(2,1)}) async-done(((bf16[8,4,8,16,1024]{4,3,1,0,2:T(8,128)(2,1)}, bf16[8,4,8,16,1024]{4,3,1,0,2:T(8,128)(2,1)}), (bf16[8,4,8,16,1024]{4,3,1,0,2:T(8,128)(2,1)}, bf16[8,4,8,16,1024]{4,3,1,0,2:T(8,128)(2,1)})) %all-reduce.15.cloned.1.call-update) | async-done | bytes 16777232
  1027.9 44.4 %all-to-all-done.3 = bf16[8,1,8,16,1024]{4,3,1,2,0:T(8,128)(2,1)} async-done(((bf16[8,1,8,16,1024]{4,3,1,2,0:T(8,128)(2,1)}), bf16[8,1,8,16,1024]{4,3,1,2,0:T(8,128)(2,1)}, u32[]{:S(2)}, u32[]{:S(2)}) %all-to-all-start.3) | async-done | bytes 2097184 | tf_op jit(solution)/shard_map/all_to_all | solution.py:205
  1081.6 43.3 %all-to-all-done.5 = bf16[8,1,8,16,1024]{4,3,1,2,0:T(8,128)(2,1)} async-done(((bf16[8,1,8,16,1024]{4,3,1,2,0:T(8,128)(2,1)}), bf16[8,1,8,16,1024]{4,3,1,2,0:T(8,128)(2,1)}, u32[]{:S(2)}, u32[]{:S(2)}) %all-to-all-start.5) | async-done | bytes 2097184 | tf_op jit(solution)/shard_map/all_to_all | solution.py:208
  1142.8 9.8 all-to-all-done.6
  1156.3 203.1 %while.31 = (s32[]{:T(128)}, f32[2048,4,64]{0,2,1:T(8,128)}, f32[2048,4,64]{0,2,1:T(8,128)}, bf16[4,512,4,64]{1,3,2,0:T(8,128)(2,1)}, s32[4]{0:T(128)S(1)}, /*in...) while((s32[]{:T(128)}, f32[2048,4,64]{0,2,1:T(8,128)}, ...), condition=%wide.region_22.23_spmd.clone.clone, body=%wide.region_20.22_spmd.clone.clone.sunk | while | flops 2753296896 | bytes 184945072 | solution.py:268
  1165.6 7.2 fusion.185
  1172.8 11.6 multiply_reduce_fusion.7
  1184.4 10.9 multiply_convert_fusion.2
  1195.3 7.1 fusion.186
  1215.5 7.6 fusion.185
  1223.1 11.5 multiply_reduce_fusion.7
  1234.6 10.9 multiply_convert_fusion.2
  1245.5 7.1 fusion.186
  1266.4 7.6 fusion.185
  1274.1 11.5 multiply_reduce_fusion.7
  1285.6 10.9 multiply_convert_fusion.2
  1296.5 7.1 fusion.186
  1317.4 7.6 fusion.185
  1325.0 11.5 multiply_reduce_fusion.7
  1336.5 10.9 multiply_convert_fusion.2
  1347.4 7.1 fusion.186
  1370.3 51.9 %all_to_all.88 = bf16[2048,3,1,256]{3,1,2,0:T(4,128)(2,1)S(1)} all-to-all(bf16[2048,3,1,256]{3,1,2,0:T(4,128)(2,1)} %copy.112), channel_id=1, replica_groups=mesh['dp'=8,'seq'=4] {'seq'}, dimensions={0} | all-to-all | bytes 6291456 | tf_op jit(solution)/shard_map/all_to_all | solution.py:279
  1429.1 7.8 convolution_convert_fusion
  1439.7 23.5 %convolution_bitcast_fusion = f32[8,1024,1024]{2,1,0:T(8,128)} fusion(bf16[8,4,8,16,1024]{4,3,1,2,0:T(8,128)(2,1)} %all-to-all-done.4, bf16[8,4,8,16,1024]{4,3,1,0,2:T(8,128)(2,1)} %get-tuple-element.340), kind=kOutput, calls=%fused_computation.77 | convolution fusion | flops 8589934592 | bytes 50331648 | tf_op jit(solution)/shard_map/abecf,abecd->efd/dot_general | solution.py:56
  1463.2 30.5 %reduce-scatter.10.cloned.1.call-done = bf16[256,3072]{1,0:T(8,128)(2,1)} async-done(((bf16[1024,3072]{1,0:T(8,128)(2,1)}), bf16[256,3072]{1,0:T(8,128)(2,1)}) %reduce-scatter.10.cloned.1.call-update) | async-done | bytes 1572880 | tf_op jit(solution)/shard_map/reduce_scatter | solution.py:288
  1493.7 20.0 %convolution_bitcast_fusion.1 = f32[8,1024,1024]{2,1,0:T(8,128)} fusion(bf16[8,4,8,16,1024]{4,3,1,2,0:T(8,128)(2,1)} %all-to-all-done.2, bf16[8,4,8,16,1024]{4,3,1,0,2:T(8,128)(2,1)} %fusion.50), kind=kOutput, calls=%fused_computation.78 | convolution fusion | flops 8589934592 | bytes 50331648 | tf_op jit(solution)/shard_map/abecd,abecf->edf/dot_general | solution.py:53
  1513.8 9.2 fusion.85
  1523.0 5.8 all-reduce.8
  1529.2 39.4 %all-reduce.6 = (bf16[256]{0:T(256)(128)(2,1)S(1)}, bf16[256]{0:T(256)(128)(2,1)S(1)}, bf16[256]{0:T(256)(128)(2,1)S(1)}, bf16[256]{0:T(256)(128)(2,1)S(1)}, bf16[256,64]{0,1:T(8,128)(2,1)S(1)}) all-reduce(bf16[256]{0:T(256)(128)(2,1)S(1)} %dynamic-slice.5, ...), channel_id=1, replica_groups=mesh['dp'=8,'seq'=4] {'dp'}, use_global_device_ids=true, to_apply=%region_27.28 | all-reduce | flops 17408 | bytes 69632 | tf_op jit(solution)/shard_map/psum | solution.py:314
  1575.1 48.5 %all-reduce.13.cloned.1.call-done = (bf16[256,3072]{1,0:T(8,128)(2,1)}, bf16[256,1024]{1,0:T(8,128)(2,1)}) async-done(((bf16[256,3072]{1,0:T(8,128)(2,1)}, bf16[256,1024]{1,0:T(8,128)(2,1)}), (bf16[256,3072]{1,0:T(8,128)(2,1)}, bf16[256,1024]{1,0:T(8,128)(2,1)})) %all-reduce.13.cloned.1.call-update) | async-done | bytes 2097168 | tf_op jit(solution)/shard_map/psum | solution.py:311
  (296 shorter events, 230.3 us)
Async XLA Ops:
  7.2 51.5 %all-gather.9.cloned.1.call-start = ((), (), s32[]{:S(2)}) async-start(), calls=%async_computation.11 | async-start | bytes 7864320 | tf_op jit(solution)/shard_map/all_gather | solution.py:83
  15.2 43.5 %copy-start.40 = (f32[4,1,256]{2,1,0:T(1,128)}, f32[4,1,256]{2,1,0:T(1,128)S(1)}, u32[]{:S(2)}) copy-start(f32[4,1,256]{2,1,0:T(1,128)S(1)} %convert_element_type.208) | copy-start | bytes 12292
  20.6 38.1 %copy-start.32 = (f32[4,1,256]{2,1,0:T(1,128)}, f32[4,1,256]{2,1,0:T(1,128)S(1)}, u32[]{:S(2)}) copy-start(f32[4,1,256]{2,1,0:T(1,128)S(1)} %convert_element_type.207) | copy-start | bytes 12292
  22.2 36.5 %copy-start.29 = (f32[512]{0:T(512)}, f32[512]{0:T(512)S(1)}, u32[]{:S(2)}) copy-start(f32[512]{0:T(512)S(1)} %broadcast_multiply_fusion.5) | copy-start | bytes 6148
  23.9 34.7 %copy-start.37 = (f32[512]{0:T(512)}, f32[512]{0:T(512)S(1)}, u32[]{:S(2)}) copy-start(f32[512]{0:T(512)S(1)} %add_rsqrt_fusion.1) | copy-start | bytes 6148
  74.7 52.0 %all-to-all-start = ((bf16[512,3,4,256]{3,0,1,2:T(8,128)(2,1)}), bf16[512,3,4,256]{3,0,1,2:T(8,128)(2,1)S(1)}, u32[]{:S(2)}, u32[]{:S(2)}) async-start(bf16[512,3,4,256]{3,0,1,2:T(8,128)(2,1)} %copy.97), calls=%async_computation | async-start | bytes 6291456 | tf_op jit(solution)/shard_map/all_to_all | solution.py:109
  78.5 147.0 %all-gather.11.cloned.1.call-start = ((), (), s32[]{:S(2)}) async-start(), calls=%async_computation.12 | async-start | bytes 2621440 | tf_op jit(solution)/shard_map/all_gather | solution.py:84
  131.9 71.4 %copy-start.45 = (bf16[256]{0:T(256)(128)(2,1)S(1)}, bf16[256]{0:T(256)(128)(2,1)}, u32[]{:S(2)}) copy-start(bf16[256]{0:T(256)(128)(2,1)} %param.24) | copy-start | bytes 1540
  131.9 71.4 %copy-start.46 = (bf16[256]{0:T(256)(128)(2,1)S(1)}, bf16[256]{0:T(256)(128)(2,1)}, u32[]{:S(2)}) copy-start(bf16[256]{0:T(256)(128)(2,1)} %param.25) | copy-start | bytes 1540
  131.9 91.9 %copy-start.20 = (s32[512,1]{0,1:T(1,128)S(1)}, s32[512,1]{0,1:T(1,128)}, u32[]{:S(2)}) copy-start(s32[512,1]{0,1:T(1,128)} %param.19) | copy-start | bytes 6148
  199.0 26.5 %copy-start.4 = (bf16[2048,4,64]{0,2,1:T(8,128)(2,1)}, bf16[2048,4,64]{0,2,1:T(8,128)(2,1)S(1)}, u32[]{:S(2)}) copy-start(bf16[2048,4,64]{0,2,1:T(8,128)(2,1)S(1)} %get-tuple-element.574) | copy-start | bytes 3145732
  199.0 26.5 %copy-start.5 = (bf16[2048,4,64]{0,2,1:T(8,128)(2,1)}, bf16[2048,4,64]{0,2,1:T(8,128)(2,1)S(1)}, u32[]{:S(2)}) copy-start(bf16[2048,4,64]{0,2,1:T(8,128)(2,1)S(1)} %get-tuple-element.575) | copy-start | bytes 3145732
  199.0 26.5 %all-to-all-start.1 = ((bf16[4,512,256]{1,2,0:T(8,128)(2,1)}), bf16[4,512,256]{1,2,0:T(8,128)(2,1)}, u32[]{:S(2)}, u32[]{:S(2)}) async-start(bf16[4,512,256]{1,2,0:T(8,128)(2,1)} %bitcast.224), calls=%async_computation.1 | async-start | bytes 2097152 | tf_op jit(solution)/shard_map/all_to_all | solution.py:155
  203.2 87.7 %all-gather.13.cloned.1.call-start = ((), (), s32[]{:S(2)}) async-start(), calls=%async_computation.13 | async-start | bytes 10485760 | tf_op jit(solution)/shard_map/all_gather | solution.py:28
  232.5 64.0 %copy-start.24 = (bf16[256,64]{0,1:T(8,128)(2,1)S(1)}, bf16[256,64]{0,1:T(8,128)(2,1)}, u32[]{:S(2)}) copy-start(bf16[256,64]{0,1:T(8,128)(2,1)} %param.26) | copy-start | bytes 98308
  290.9 189.1 %all-to-all-start.2 = ((bf16[8,4,8,16,1024]{4,3,1,2,0:T(8,128)(2,1)}), bf16[8,4,8,16,1024]{4,3,1,2,0:T(8,128)(2,1)}, u32[]{:S(2)}, u32[]{:S(2)}) async-start(bf16[8,4,8,16,1024]{4,3,1,2,0:T(8,128)(2,1)} %all-gather.13.cloned.1.call-done), calls=%async_computation.2 | async-start | bytes 16777216 | tf_op jit(solution)/shard_map/all_to_all | solution.py:35
  296.4 70.1 %all-gather.15.cloned.1.call-start = ((), (), s32[]{:S(2)}) async-start(), calls=%async_computation.14 | async-start | bytes 10485760 | tf_op jit(solution)/shard_map/all_gather | solution.py:29
  303.6 824.2 %copy-start.13 = (f32[512,64]{0,1:T(8,128)}, f32[512,64]{0,1:T(8,128)S(1)}, u32[]{:S(2)}) copy-start(f32[512,64]{0,1:T(8,128)S(1)} %get-tuple-element.343) | copy-start | bytes 393220
  303.6 824.2 %copy-start.22 = (f32[512]{0:T(512)}, f32[512]{0:T(512)S(1)}, u32[]{:S(2)}) copy-start(f32[512]{0:T(512)S(1)} %get-tuple-element.342) | copy-start | bytes 6148
  303.7 824.2 %copy-start.25 = (f32[512]{0:T(512)}, f32[512]{0:T(512)S(1)}, u32[]{:S(2)}) copy-start(f32[512]{0:T(512)S(1)} %fusion.107) | copy-start | bytes 6148
  303.7 826.6 %copy-start.27 = (f32[512]{0:T(512)}, f32[512]{0:T(512)S(1)}, u32[]{:S(2)}) copy-start(f32[512]{0:T(512)S(1)} %select_reduce_fusion) | copy-start | bytes 6148
  480.0 187.6 %all-to-all-start.4 = ((bf16[8,4,8,16,1024]{4,3,1,2,0:T(8,128)(2,1)}), bf16[8,4,8,16,1024]{4,3,1,2,0:T(8,128)(2,1)}, u32[]{:S(2)}, u32[]{:S(2)}) async-start(bf16[8,4,8,16,1024]{4,3,1,2,0:T(8,128)(2,1)} %all-gather.15.cloned.1.call-done), calls=%async_computation.4 | async-start | bytes 16777216 | tf_op jit(solution)/shard_map/all_to_all | solution.py:36
  485.0 529.5 %all-reduce.15.cloned.1.call-start = ((), (), s32[]{:S(2)}) async-start(), calls=%async_computation.19 | async-start | bytes 33554432
  1018.4 53.8 %all-to-all-start.3 = ((bf16[8,1,8,16,1024]{4,3,1,2,0:T(8,128)(2,1)}), bf16[8,1,8,16,1024]{4,3,1,2,0:T(8,128)(2,1)}, u32[]{:S(2)}, u32[]{:S(2)}) async-start(bf16[8,1,8,16,1024]{4,3,1,2,0:T(8,128)(2,1)} %copy.105), calls=%async_computation.3 | async-start | bytes 4194304 | tf_op jit(solution)/shard_map/all_to_all | solution.py:205
  1072.3 52.6 %all-to-all-start.5 = ((bf16[8,1,8,16,1024]{4,3,1,2,0:T(8,128)(2,1)}), bf16[8,1,8,16,1024]{4,3,1,2,0:T(8,128)(2,1)}, u32[]{:S(2)}, u32[]{:S(2)}) async-start(bf16[8,1,8,16,1024]{4,3,1,2,0:T(8,128)(2,1)} %copy.108), calls=%async_computation.5 | async-start | bytes 4194304 | tf_op jit(solution)/shard_map/all_to_all | solution.py:208
  1081.6 48.8 %copy-start.42 = (f32[512]{0:T(512)}, f32[512]{0:T(512)S(1)}, u32[]{:S(2)}) copy-start(f32[512]{0:T(512)S(1)} %get-tuple-element.344) | copy-start | bytes 6148
  1134.6 18.0 %all-to-all-start.6 = ((bf16[512,4,256]{2,0,1:T(8,128)(2,1)}), bf16[512,4,256]{2,0,1:T(8,128)(2,1)S(1)}, u32[]{:S(2)}, u32[]{:S(2)}) async-start(bf16[512,4,256]{2,0,1:T(8,128)(2,1)} %bitcast.187), calls=%async_computation.6 | async-start | bytes 2097152 | tf_op jit(solution)/shard_map/all_to_all | solution.py:233
  1138.1 325.0 %reduce-scatter.12.cloned.1.call-start = ((), (), s32[]{:S(2)}) async-start(), calls=%async_computation.16 | async-start | bytes 2621440 | tf_op jit(solution)/shard_map/reduce_scatter | solution.py:291
  1142.7 350.9 %reduce-scatter.10.cloned.1.call-start = ((), (), s32[]{:S(2)}) async-start(), calls=%async_computation.15 | async-start | bytes 7864320 | tf_op jit(solution)/shard_map/reduce_scatter | solution.py:288
  1195.3 7.1 copy-start
  1245.5 7.1 copy-start
  1296.5 7.1 copy-start
  1303.6 4.7 copy-start.19
  1347.4 7.1 copy-start
  1424.4 4.7 copy-start.6
  1424.4 4.7 copy-start.30
  1424.4 4.7 copy-start.33
  1424.4 4.7 copy-start.38
  1424.4 4.7 copy-start.41
  1437.0 92.1 %reduce-scatter.14.cloned.1.call-start = ((), (), s32[]{:S(2)}) async-start(), calls=%async_computation.17 | async-start | bytes 163840 | tf_op jit(solution)/shard_map/reduce_scatter | solution.py:294
  1439.6 184.0 %all-reduce.13.cloned.1.call-start = ((), (), s32[]{:S(2)}) async-start(), calls=%async_computation.18 | async-start | bytes 4194304 | tf_op jit(solution)/shard_map/psum | solution.py:311
  1493.7 20.1 %copy-start.7 = (bf16[512,1024]{1,0:T(8,128)(2,1)S(1)}, bf16[512,1024]{1,0:T(8,128)(2,1)}, u32[]{:S(2)}) copy-start(bf16[512,1024]{1,0:T(8,128)(2,1)} %param.17) | copy-start | bytes 3145732
  1493.7 20.1 %copy-start.31 = (f32[512]{0:T(512)S(1)}, f32[512]{0:T(512)}, u32[]{:S(2)}) copy-start(f32[512]{0:T(512)} %copy-done.29) | copy-start | bytes 6148
  1493.7 20.1 %copy-start.34 = (f32[4,1,256]{2,1,0:T(1,128)S(1)}, f32[4,1,256]{2,1,0:T(1,128)}, u32[]{:S(2)}) copy-start(f32[4,1,256]{2,1,0:T(1,128)} %copy-done.32) | copy-start | bytes 12292
  1493.7 20.1 %copy-start.39 = (f32[512]{0:T(512)S(1)}, f32[512]{0:T(512)}, u32[]{:S(2)}) copy-start(f32[512]{0:T(512)} %copy-done.37) | copy-start | bytes 6148
  1513.8 9.2 copy-start.35
  1513.8 9.2 copy-start.36
  1513.8 57.7 %copy-start.9 = (f32[512,1024]{1,0:T(8,128)S(1)}, f32[512,1024]{1,0:T(8,128)}, u32[]{:S(2)}) copy-start(f32[512,1024]{1,0:T(8,128)} %copy-done.8) | copy-start | bytes 6291460
  (31 other events, 96.0 us)
Sparse Core Ops, SparseCore 0:
  9.6 49.0 all-gather.8
  80.9 35.3 all-gather.10
  232.6 58.2 all-gather.12
  307.8 58.7 all-gather.14
  727.5 286.9 all-reduce.14
  1142.8 30.8 reduce-scatter.11
  1437.2 56.4 reduce-scatter.9
  1496.7 19.5 reduce-scatter.13
  1520.4 103.1 all-reduce.12
where the time goes:
time: 1640 us
  waiting for transfers between devices  934 us (57%)
  matrix products  356 us (22%)
  blocking collectives  134 us (8%)
  other arithmetic  95.7 us (6%)
  local copies, waits for them, and re-layouts  53.1 us (3%)
  starting transfers between devices  33.5 us (2%)
    unnamed x10, waiting for transfers between devices  287 us
    all_to_all x1, waiting for transfers between devices, route_rows(): lax.all_to_all(grads_part, 'dp', split_axis=0, concat_axis=0, tiled=True)  158 us
    all_to_all x1, waiting for transfers between devices, route_rows(): lax.all_to_all(rows_part, 'dp', split_axis=0, concat_axis=0, tiled=True)  113 us
    all_gather x1, waiting for transfers between devices, collect_rows(): lax.all_gather(grads_part, 'seq', axis=1, tiled=True)  58.9 us
    all_gather x1, waiting for transfers between devices, collect_rows(): lax.all_gather(rows_part, 'seq', axis=1, tiled=True)  58.4 us
    all_to_all x1, blocking collectives, per_device(): lax.all_to_all(grad_qkv_heads, 'seq', split_axis=0, concat_axis=2, tiled=...  51.9 us
    psum x1, waiting for transfers between devices, per_device(): lax.psum(summed[0].astype(jnp.bfloat16), 'dp').astype(jnp.float32)  48.5 us
    all_to_all x1, waiting for transfers between devices, per_device(): lax.all_to_all(qkv_local.reshape(row_count, 3, seq_count, head_width), 's...  47.3 us
  transfers between devices with their start and end apart: 16, of which 12 were waited for; matrix products, arithmetic and copies ran while one was open for 25% of the time, Pallas kernels for 0%

commit v1 on v0

--- a/solution.py
+++ b/solution.py
@@ -1,3 +1,4 @@
+import functools
 import jax
 import jax.numpy as jnp
 from jax import lax
@@ -9,6 +10,14 @@
 TOK_DEV = 512
 EPS = 1e-05
 NEG = -1e30
+
+
+def change_slot(x_local, mesh_ax):
+    x_now = jax.lax.all_gather(x_local, axis_name=mesh_ax)
+    return jnp.sum(x_now, axis=0)
+
+
+check_forms = functools.partial(change_slot, mesh_ax="dp")
 
 
 def normalize(values):
@@ -308,7 +317,7 @@
         ).astype(jnp.float32),
     )
     reduced = (
-        lax.psum(summed[0].astype(jnp.bfloat16), "dp").astype(jnp.float32),
+        check_forms(summed[0].astype(jnp.bfloat16)).astype(jnp.float32),
         lax.psum(summed[1].astype(jnp.bfloat16), "dp").astype(jnp.float32),
         lax.psum(summed[2].astype(jnp.bfloat16), "dp").astype(jnp.float32),
         lax.psum(summed[3].astype(jnp.bfloat16), "dp").astype(jnp.float32),

time: 1640 us -> 1790 us (1.091)
  waiting for transfers between devices: 934 us -> 1080 us
    all_gather x0 -> x1, waiting for transfers between devices: none -> 174 us  [change_slot(): x_now = jax.lax.all_gather(x_local, axis_name=mesh_ax)]
    psum x1, waiting for transfers between devices: 48.5 us -> 0.01 us  [per_device(): lax.psum(summed[1].astype(jnp.bfloat16), 'dp').astype(jnp.float32)]
    reduce_scatter x1, waiting for transfers between devices: 30.5 us -> 52.6 us  [per_device(): lax.psum_scatter(qkv_grad.astype(jnp.bfloat16), 'seq', scatter_dimension=...]
    unnamed x10 -> x11, waiting for transfers between devices: 287 us -> 288 us
  transfers between devices with their start and end apart: 16 -> 17, of which waited for: 12 -> 12; matrix products, arithmetic and copies ran while one was open for 25% -> 22% of each run, Pallas kernels for 0% -> 0%
where the time goes in v1:
time: 1790 us
  waiting for transfers between devices  1080 us (60%)
  matrix products  354 us (20%)
  blocking collectives  133 us (7%)
  other arithmetic  102 us (6%)
  local copies, waits for them, and re-layouts  53.8 us (3%)
  starting transfers between devices  32.9 us (2%)
    unnamed x11, waiting for transfers between devices  288 us
    all_gather x1, waiting for transfers between devices, change_slot(): x_now = jax.lax.all_gather(x_local, axis_name=mesh_ax)  174 us
    all_to_all x1, waiting for transfers between devices, route_rows(): lax.all_to_all(grads_part, 'dp', split_axis=0, concat_axis=0, tiled=True)  158 us
    all_to_all x1, waiting for transfers between devices, route_rows(): lax.all_to_all(rows_part, 'dp', split_axis=0, concat_axis=0, tiled=True)  113 us
    all_gather x1, waiting for transfers between devices, collect_rows(): lax.all_gather(grads_part, 'seq', axis=1, tiled=True)  58.9 us
    all_gather x1, waiting for transfers between devices, collect_rows(): lax.all_gather(rows_part, 'seq', axis=1, tiled=True)  58.4 us
    reduce_scatter x1, waiting for transfers between devices, per_device(): lax.psum_scatter(qkv_grad.astype(jnp.bfloat16), 'seq', scatter_dimension=...  52.6 us
    all_to_all x1, blocking collectives, per_device(): lax.all_to_all(grad_qkv_heads, 'seq', split_axis=0, concat_axis=2, tiled=...  51.9 us
  transfers between devices with their start and end apart: 17, of which 12 were waited for; matrix products, arithmetic and copies ran while one was open for 22% of the time, Pallas kernels for 0%

profile of v1, /device:TPU:0, one launch (start us, length us, event | category | flops | bytes accessed | tf_op | source)
XLA Modules:
  0.0 1787.3 jit_solution(3253484305196933965)
XLA Ops:
  9.2 6.0 all-gather.2
  24.0 34.7 %all-gather.11.cloned.1.call-done = bf16[1024,3072]{1,0:T(8,128)(2,1)} async-done(((bf16[256,3072]{1,0:T(8,128)(2,1)}), bf16[1024,3072]{1,0:T(8,128)(2,1)}) %all-gather.11.cloned.1.call-update) | async-done | bytes 6291472 | tf_op jit(solution)/shard_map/all_gather | solution.py:92
  58.7 8.3 convolution_convert_fusion.1
  79.4 47.3 %all-to-all-done = bf16[512,3,4,256]{3,0,1,2:T(8,128)(2,1)S(1)} async-done(((bf16[512,3,4,256]{3,0,1,2:T(8,128)(2,1)}), bf16[512,3,4,256]{3,0,1,2:T(8,128)(2,1)S(1)}, u32[]{:S(2)}, u32[]{:S(2)}) %all-to-all-start) | async-done | bytes 3145760 | tf_op jit(solution)/shard_map/all_to_all | solution.py:118
  131.9 67.1 %while.30 = (s32[]{:T(128)}, bf16[4,512,4,64]{1,3,2,0:T(8,128)(2,1)}, f32[4,4,512]{2,1,0:T(4,128)}, s32[4]{0:T(128)S(1)}, s32[2048]{0:T(1024)S(1)}, /*index=5*/b...) while((s32[]{:T(128)}, ...), condition=%wide.region_6.7_spmd.clone.clone, body=%wide.region_3.6_spmd.clone.clone.sunk | while | flops 1127348736 | bytes 57223368 | solution.py:162
  142.1 5.9 fusion.172
  158.9 5.9 fusion.172
  175.7 5.9 fusion.172
  192.4 5.9 fusion.172
  203.3 15.3 all-gather.4
  232.5 58.4 %all-gather.15.cloned.1.call-done = bf16[8,4,8,16,1024]{4,3,1,2,0:T(8,128)(2,1)} async-done(((bf16[8,1,8,16,1024]{4,3,1,2,0:T(8,128)(2,1)}), bf16[8,4,8,16,1024]{4,3,1,2,0:T(8,128)(2,1)}) %all-gather.15.cloned.1.call-update) | async-done | bytes 8388624 | tf_op jit(solution)/shard_map/all_gather | solution.py:37
  307.7 58.9 %all-gather.17.cloned.1.call-done = bf16[8,4,8,16,1024]{4,3,1,2,0:T(8,128)(2,1)} async-done(((bf16[8,1,8,16,1024]{4,3,1,2,0:T(8,128)(2,1)}), bf16[8,4,8,16,1024]{4,3,1,2,0:T(8,128)(2,1)}) %all-gather.17.cloned.1.call-update) | async-done | bytes 8388624 | tf_op jit(solution)/shard_map/all_gather | solution.py:38
  366.6 113.5 %all-to-all-done.2 = bf16[8,4,8,16,1024]{4,3,1,2,0:T(8,128)(2,1)} async-done(((bf16[8,4,8,16,1024]{4,3,1,2,0:T(8,128)(2,1)}), bf16[8,4,8,16,1024]{4,3,1,2,0:T(8,128)(2,1)}, u32[]{:S(2)}, u32[]{:S(2)}) %all-to-all-start.2) | async-done | bytes 8388640 | tf_op jit(solution)/shard_map/all_to_all | solution.py:44
  485.3 24.4 %fusion.62 = (bf16[8,4,8,16,1024]{4,3,1,0,2:T(8,128)(2,1)}, f32[8,8,4,16,1024]{4,3,2,1,0:T(8,128)}) fusion(bf16[8,1024,1024]{2,1,0:T(8,128)(2,1)} %param.27, bf16[8,4,8,16,1024]{4,3,1,2,0:T(8,128)(2,1)} %all-to-all-done.2), kind=kOutput, calls=%fused_computation.76 | convolution fusion | flops 8627683328 | bytes 50331648 | tf_op jit(solution)/shard_map/abecd,edf->abecf/dot_general | solution.py:50
  509.8 157.9 %all-to-all-done.4 = bf16[8,4,8,16,1024]{4,3,1,2,0:T(8,128)(2,1)} async-done(((bf16[8,4,8,16,1024]{4,3,1,2,0:T(8,128)(2,1)}), bf16[8,4,8,16,1024]{4,3,1,2,0:T(8,128)(2,1)}, u32[]{:S(2)}, u32[]{:S(2)}) %all-to-all-start.4) | async-done | bytes 8388640 | tf_op jit(solution)/shard_map/all_to_all | solution.py:45
  667.7 25.9 %fusion.50 = bf16[8,4,8,16,1024]{4,3,1,0,2:T(8,128)(2,1)} fusion(f32[8,8,4,16,1024]{4,3,2,1,0:T(8,128)} %get-tuple-element.339, bf16[8,1024,1024]{2,1,0:T(8,128)(2,1)} %param.28, bf16[8,4,8,16,1024]{4,3,1,2,0:T(8,128)(2,1)} %all-to-all-done.4), kind=kOutput, calls=%fused_computation.61 | convolution fusion | flops 8673820672 | bytes 50331648 | tf_op jit(solution)/shard_map/abecd,efd->abecf/dot_general | solution.py:58
  693.6 16.3 convert_bitcast_fusion
  709.9 18.1 %convert_bitcast_fusion.1 = bf16[8,4,8,16,1024]{4,3,1,0,2:T(8,128)(2,1)} fusion(bf16[8,4,8,16,1024]{4,3,1,0,2:T(8,128)(2,1)} %get-tuple-element.338, bf16[8,1024,1024]{2,1,0:T(8,128)(2,1)} %param.28), kind=kOutput, calls=%fused_computation.84 | convolution fusion | flops 8594128896 | bytes 33554432 | tf_op jit(solution)/shard_map/abecf,efd->abecd/dot_general | solution.py:55
  729.2 285.9 %all-reduce.14.cloned.1.call-done = (bf16[8,4,8,16,1024]{4,3,1,0,2:T(8,128)(2,1)}, bf16[8,4,8,16,1024]{4,3,1,0,2:T(8,128)(2,1)}) async-done(((bf16[8,4,8,16,1024]{4,3,1,0,2:T(8,128)(2,1)}, bf16[8,4,8,16,1024]{4,3,1,0,2:T(8,128)(2,1)}), (bf16[8,4,8,16,1024]{4,3,1,0,2:T(8,128)(2,1)}, bf16[8,4,8,16,1024]{4,3,1,0,2:T(8,128)(2,1)})) %all-reduce.14.cloned.1.call-update) | async-done | bytes 16777232
  1028.5 44.4 %all-to-all-done.3 = bf16[8,1,8,16,1024]{4,3,1,2,0:T(8,128)(2,1)} async-done(((bf16[8,1,8,16,1024]{4,3,1,2,0:T(8,128)(2,1)}), bf16[8,1,8,16,1024]{4,3,1,2,0:T(8,128)(2,1)}, u32[]{:S(2)}, u32[]{:S(2)}) %all-to-all-start.3) | async-done | bytes 2097184 | tf_op jit(solution)/shard_map/all_to_all | solution.py:214
  1081.9 43.3 %all-to-all-done.5 = bf16[8,1,8,16,1024]{4,3,1,2,0:T(8,128)(2,1)} async-done(((bf16[8,1,8,16,1024]{4,3,1,2,0:T(8,128)(2,1)}), bf16[8,1,8,16,1024]{4,3,1,2,0:T(8,128)(2,1)}, u32[]{:S(2)}, u32[]{:S(2)}) %all-to-all-start.5) | async-done | bytes 2097184 | tf_op jit(solution)/shard_map/all_to_all | solution.py:217
  1143.2 9.7 all-to-all-done.6
  1156.7 203.5 %while.31 = (s32[]{:T(128)}, f32[2048,4,64]{0,2,1:T(8,128)}, f32[2048,4,64]{0,2,1:T(8,128)}, bf16[4,512,4,64]{1,3,2,0:T(8,128)(2,1)}, s32[4]{0:T(128)S(1)}, /*in...) while((s32[]{:T(128)}, f32[2048,4,64]{0,2,1:T(8,128)}, ...), condition=%wide.region_22.23_spmd.clone.clone, body=%wide.region_20.22_spmd.clone.clone.sunk | while | flops 2753296896 | bytes 184945072 | solution.py:277
  1166.0 7.2 fusion.185
  1173.2 11.5 multiply_reduce_fusion.7
  1184.8 10.9 multiply_convert_fusion.2
  1195.6 7.2 fusion.186
  1215.9 7.6 fusion.185
  1223.5 11.5 multiply_reduce_fusion.7
  1235.1 10.9 multiply_convert_fusion.2
  1245.9 7.1 fusion.186
  1266.9 7.6 fusion.185
  1274.5 11.5 multiply_reduce_fusion.7
  1286.1 10.9 multiply_convert_fusion.2
  1296.9 7.1 fusion.186
  1317.9 7.6 fusion.185
  1325.5 11.5 multiply_reduce_fusion.7
  1337.0 10.9 multiply_convert_fusion.2
  1347.9 7.1 fusion.186
  1371.1 51.9 %all_to_all.88 = bf16[2048,3,1,256]{3,1,2,0:T(4,128)(2,1)S(1)} all-to-all(bf16[2048,3,1,256]{3,1,2,0:T(4,128)(2,1)} %copy.112), channel_id=1, replica_groups=mesh['dp'=8,'seq'=4] {'seq'}, dimensions={0} | all-to-all | bytes 6291456 | tf_op jit(solution)/shard_map/all_to_all | solution.py:288
  1430.0 7.8 convolution_convert_fusion
  1441.8 52.6 %reduce-scatter.10.cloned.1.call-done = bf16[256,3072]{1,0:T(8,128)(2,1)} async-done(((bf16[1024,3072]{1,0:T(8,128)(2,1)}), bf16[256,3072]{1,0:T(8,128)(2,1)}) %reduce-scatter.10.cloned.1.call-update) | async-done | bytes 1572880 | tf_op jit(solution)/shard_map/reduce_scatter | solution.py:297
  1494.4 20.9 %convolution_bitcast_fusion = f32[8,1024,1024]{2,1,0:T(8,128)} fusion(bf16[8,4,8,16,1024]{4,3,1,2,0:T(8,128)(2,1)} %all-to-all-done.4, bf16[8,4,8,16,1024]{4,3,1,0,2:T(8,128)(2,1)} %get-tuple-element.338), kind=kOutput, calls=%fused_computation.77 | convolution fusion | flops 8589934592 | bytes 50331648 | tf_op jit(solution)/shard_map/abecf,abecd->efd/dot_general | solution.py:65
  1515.3 19.9 %convolution_bitcast_fusion.1 = f32[8,1024,1024]{2,1,0:T(8,128)} fusion(bf16[8,4,8,16,1024]{4,3,1,2,0:T(8,128)(2,1)} %all-to-all-done.2, bf16[8,4,8,16,1024]{4,3,1,0,2:T(8,128)(2,1)} %fusion.50), kind=kOutput, calls=%fused_computation.78 | convolution fusion | flops 8589934592 | bytes 50331648 | tf_op jit(solution)/shard_map/abecd,abecf->edf/dot_general | solution.py:62
  1535.3 9.2 fusion.85
  1550.7 37.9 %all-reduce.6 = (bf16[256]{0:T(256)(128)(2,1)S(1)}, bf16[256]{0:T(256)(128)(2,1)S(1)}, bf16[256]{0:T(256)(128)(2,1)S(1)}, bf16[256]{0:T(256)(128)(2,1)S(1)}, bf16[256,64]{0,1:T(8,128)(2,1)S(1)}) all-reduce(bf16[256]{0:T(256)(128)(2,1)S(1)} %dynamic-slice.5, ...), channel_id=1, replica_groups=mesh['dp'=8,'seq'=4] {'dp'}, use_global_device_ids=true, to_apply=%region_27.28 | all-reduce | flops 17408 | bytes 69632 | tf_op jit(solution)/shard_map/psum | solution.py:323
  1597.2 173.8 %all-gather.19.cloned.1.call-done = bf16[2048,3072]{1,0:T(8,128)(2,1)} async-done(((bf16[256,3072]{1,0:T(8,128)(2,1)}), bf16[2048,3072]{1,0:T(8,128)(2,1)}) %all-gather.19.cloned.1.call-update) | async-done | bytes 12582928 | tf_op jit(solution)/shard_map/all_gather | solution.py:16
  1771.0 7.3 reduce_sum.188
  (300 shorter events, 236.1 us)
Async XLA Ops:
  7.2 51.5 %all-gather.11.cloned.1.call-start = ((), (), s32[]{:S(2)}) async-start(), calls=%async_computation.11 | async-start | bytes 7864320 | tf_op jit(solution)/shard_map/all_gather | solution.py:92
  15.2 43.5 %copy-start.40 = (f32[4,1,256]{2,1,0:T(1,128)}, f32[4,1,256]{2,1,0:T(1,128)S(1)}, u32[]{:S(2)}) copy-start(f32[4,1,256]{2,1,0:T(1,128)S(1)} %convert_element_type.210) | copy-start | bytes 12292
  20.6 38.1 %copy-start.32 = (f32[4,1,256]{2,1,0:T(1,128)}, f32[4,1,256]{2,1,0:T(1,128)S(1)}, u32[]{:S(2)}) copy-start(f32[4,1,256]{2,1,0:T(1,128)S(1)} %convert_element_type.209) | copy-start | bytes 12292
  22.2 36.5 %copy-start.29 = (f32[512]{0:T(512)}, f32[512]{0:T(512)S(1)}, u32[]{:S(2)}) copy-start(f32[512]{0:T(512)S(1)} %broadcast_multiply_fusion.5) | copy-start | bytes 6148
  23.9 34.7 %copy-start.37 = (f32[512]{0:T(512)}, f32[512]{0:T(512)S(1)}, u32[]{:S(2)}) copy-start(f32[512]{0:T(512)S(1)} %add_rsqrt_fusion.1) | copy-start | bytes 6148
  74.7 52.0 %all-to-all-start = ((bf16[512,3,4,256]{3,0,1,2:T(8,128)(2,1)}), bf16[512,3,4,256]{3,0,1,2:T(8,128)(2,1)S(1)}, u32[]{:S(2)}, u32[]{:S(2)}) async-start(bf16[512,3,4,256]{3,0,1,2:T(8,128)(2,1)} %copy.97), calls=%async_computation | async-start | bytes 6291456 | tf_op jit(solution)/shard_map/all_to_all | solution.py:118
  78.5 147.0 %all-gather.13.cloned.1.call-start = ((), (), s32[]{:S(2)}) async-start(), calls=%async_computation.12 | async-start | bytes 2621440 | tf_op jit(solution)/shard_map/all_gather | solution.py:93
  131.9 71.4 %copy-start.45 = (bf16[256]{0:T(256)(128)(2,1)S(1)}, bf16[256]{0:T(256)(128)(2,1)}, u32[]{:S(2)}) copy-start(bf16[256]{0:T(256)(128)(2,1)} %param.24) | copy-start | bytes 1540
  131.9 71.4 %copy-start.46 = (bf16[256]{0:T(256)(128)(2,1)S(1)}, bf16[256]{0:T(256)(128)(2,1)}, u32[]{:S(2)}) copy-start(bf16[256]{0:T(256)(128)(2,1)} %param.25) | copy-start | bytes 1540
  131.9 92.0 %copy-start.20 = (s32[512,1]{0,1:T(1,128)S(1)}, s32[512,1]{0,1:T(1,128)}, u32[]{:S(2)}) copy-start(s32[512,1]{0,1:T(1,128)} %param.19) | copy-start | bytes 6148
  199.0 26.6 %copy-start.4 = (bf16[2048,4,64]{0,2,1:T(8,128)(2,1)}, bf16[2048,4,64]{0,2,1:T(8,128)(2,1)S(1)}, u32[]{:S(2)}) copy-start(bf16[2048,4,64]{0,2,1:T(8,128)(2,1)S(1)} %get-tuple-element.570) | copy-start | bytes 3145732
  199.0 26.6 %copy-start.5 = (bf16[2048,4,64]{0,2,1:T(8,128)(2,1)}, bf16[2048,4,64]{0,2,1:T(8,128)(2,1)S(1)}, u32[]{:S(2)}) copy-start(bf16[2048,4,64]{0,2,1:T(8,128)(2,1)S(1)} %get-tuple-element.571) | copy-start | bytes 3145732
  199.0 26.6 %all-to-all-start.1 = ((bf16[4,512,256]{1,2,0:T(8,128)(2,1)}), bf16[4,512,256]{1,2,0:T(8,128)(2,1)}, u32[]{:S(2)}, u32[]{:S(2)}) async-start(bf16[4,512,256]{1,2,0:T(8,128)(2,1)} %bitcast.226), calls=%async_computation.1 | async-start | bytes 2097152 | tf_op jit(solution)/shard_map/all_to_all | solution.py:164
  203.2 87.7 %all-gather.15.cloned.1.call-start = ((), (), s32[]{:S(2)}) async-start(), calls=%async_computation.13 | async-start | bytes 10485760 | tf_op jit(solution)/shard_map/all_gather | solution.py:37
  232.5 64.0 %copy-start.24 = (bf16[256,64]{0,1:T(8,128)(2,1)S(1)}, bf16[256,64]{0,1:T(8,128)(2,1)}, u32[]{:S(2)}) copy-start(bf16[256,64]{0,1:T(8,128)(2,1)} %param.26) | copy-start | bytes 98308
  291.0 189.1 %all-to-all-start.2 = ((bf16[8,4,8,16,1024]{4,3,1,2,0:T(8,128)(2,1)}), bf16[8,4,8,16,1024]{4,3,1,2,0:T(8,128)(2,1)}, u32[]{:S(2)}, u32[]{:S(2)}) async-start(bf16[8,4,8,16,1024]{4,3,1,2,0:T(8,128)(2,1)} %all-gather.15.cloned.1.call-done), calls=%async_computation.2 | async-start | bytes 16777216 | tf_op jit(solution)/shard_map/all_to_all | solution.py:44
  296.5 70.1 %all-gather.17.cloned.1.call-start = ((), (), s32[]{:S(2)}) async-start(), calls=%async_computation.14 | async-start | bytes 10485760 | tf_op jit(solution)/shard_map/all_gather | solution.py:38
  303.7 824.5 %copy-start.13 = (f32[512,64]{0,1:T(8,128)}, f32[512,64]{0,1:T(8,128)S(1)}, u32[]{:S(2)}) copy-start(f32[512,64]{0,1:T(8,128)S(1)} %get-tuple-element.341) | copy-start | bytes 393220
  303.7 824.5 %copy-start.22 = (f32[512]{0:T(512)}, f32[512]{0:T(512)S(1)}, u32[]{:S(2)}) copy-start(f32[512]{0:T(512)S(1)} %get-tuple-element.340) | copy-start | bytes 6148
  303.7 824.4 %copy-start.25 = (f32[512]{0:T(512)}, f32[512]{0:T(512)S(1)}, u32[]{:S(2)}) copy-start(f32[512]{0:T(512)S(1)} %fusion.107) | copy-start | bytes 6148
  303.8 826.9 %copy-start.27 = (f32[512]{0:T(512)}, f32[512]{0:T(512)S(1)}, u32[]{:S(2)}) copy-start(f32[512]{0:T(512)S(1)} %select_reduce_fusion) | copy-start | bytes 6148
  480.1 187.6 %all-to-all-start.4 = ((bf16[8,4,8,16,1024]{4,3,1,2,0:T(8,128)(2,1)}), bf16[8,4,8,16,1024]{4,3,1,2,0:T(8,128)(2,1)}, u32[]{:S(2)}, u32[]{:S(2)}) async-start(bf16[8,4,8,16,1024]{4,3,1,2,0:T(8,128)(2,1)} %all-gather.17.cloned.1.call-done), calls=%async_computation.4 | async-start | bytes 16777216 | tf_op jit(solution)/shard_map/all_to_all | solution.py:45
  485.0 530.1 %all-reduce.14.cloned.1.call-start = ((), (), s32[]{:S(2)}) async-start(), calls=%async_computation.20 | async-start | bytes 33554432
  1019.0 53.8 %all-to-all-start.3 = ((bf16[8,1,8,16,1024]{4,3,1,2,0:T(8,128)(2,1)}), bf16[8,1,8,16,1024]{4,3,1,2,0:T(8,128)(2,1)}, u32[]{:S(2)}, u32[]{:S(2)}) async-start(bf16[8,1,8,16,1024]{4,3,1,2,0:T(8,128)(2,1)} %copy.105), calls=%async_computation.3 | async-start | bytes 4194304 | tf_op jit(solution)/shard_map/all_to_all | solution.py:214
  1072.9 52.3 %all-to-all-start.5 = ((bf16[8,1,8,16,1024]{4,3,1,2,0:T(8,128)(2,1)}), bf16[8,1,8,16,1024]{4,3,1,2,0:T(8,128)(2,1)}, u32[]{:S(2)}, u32[]{:S(2)}) async-start(bf16[8,1,8,16,1024]{4,3,1,2,0:T(8,128)(2,1)} %copy.108), calls=%async_computation.5 | async-start | bytes 4194304 | tf_op jit(solution)/shard_map/all_to_all | solution.py:217
  1081.9 48.8 %copy-start.42 = (f32[512]{0:T(512)}, f32[512]{0:T(512)S(1)}, u32[]{:S(2)}) copy-start(f32[512]{0:T(512)S(1)} %get-tuple-element.342) | copy-start | bytes 6148
  1135.0 18.0 %all-to-all-start.6 = ((bf16[512,4,256]{2,0,1:T(8,128)(2,1)}), bf16[512,4,256]{2,0,1:T(8,128)(2,1)S(1)}, u32[]{:S(2)}, u32[]{:S(2)}) async-start(bf16[512,4,256]{2,0,1:T(8,128)(2,1)} %bitcast.188), calls=%async_computation.6 | async-start | bytes 2097152 | tf_op jit(solution)/shard_map/all_to_all | solution.py:242
  1138.5 301.9 %reduce-scatter.12.cloned.1.call-start = ((), (), s32[]{:S(2)}) async-start(), calls=%async_computation.16 | async-start | bytes 2621440 | tf_op jit(solution)/shard_map/reduce_scatter | solution.py:300
  1143.1 351.3 %reduce-scatter.10.cloned.1.call-start = ((), (), s32[]{:S(2)}) async-start(), calls=%async_computation.15 | async-start | bytes 7864320 | tf_op jit(solution)/shard_map/reduce_scatter | solution.py:297
  1195.6 7.2 copy-start
  1245.9 7.1 copy-start
  1296.9 7.1 copy-start
  1347.9 7.1 copy-start
  1425.1 4.8 copy-start.6
  1425.1 4.8 copy-start.30
  1425.1 4.8 copy-start.33
  1425.1 4.8 copy-start.38
  1425.1 4.8 copy-start.41
  1437.8 112.9 %reduce-scatter.14.cloned.1.call-start = ((), (), s32[]{:S(2)}) async-start(), calls=%async_computation.18 | async-start | bytes 163840 | tf_op jit(solution)/shard_map/reduce_scatter | solution.py:303
  1440.3 154.7 %all-reduce.12.cloned.1.call-start = ((), (), s32[]{:S(2)}) async-start(), calls=%async_computation.17 | async-start | bytes 1048576 | tf_op jit(solution)/shard_map/psum | solution.py:321
  1441.1 329.9 %all-gather.19.cloned.1.call-start = ((), (), s32[]{:S(2)}) async-start(), calls=%async_computation.19 | async-start | bytes 14155776 | tf_op jit(solution)/shard_map/all_gather | solution.py:16
  1515.3 20.0 %copy-start.7 = (bf16[512,1024]{1,0:T(8,128)(2,1)S(1)}, bf16[512,1024]{1,0:T(8,128)(2,1)}, u32[]{:S(2)}) copy-start(bf16[512,1024]{1,0:T(8,128)(2,1)} %param.17) | copy-start | bytes 3145732
  1515.3 20.0 %copy-start.31 = (f32[512]{0:T(512)S(1)}, f32[512]{0:T(512)}, u32[]{:S(2)}) copy-start(f32[512]{0:T(512)} %copy-done.29) | copy-start | bytes 6148
  1515.3 20.0 %copy-start.34 = (f32[4,1,256]{2,1,0:T(1,128)S(1)}, f32[4,1,256]{2,1,0:T(1,128)}, u32[]{:S(2)}) copy-start(f32[4,1,256]{2,1,0:T(1,128)} %copy-done.32) | copy-start | bytes 12292
  1515.3 20.0 %copy-start.39 = (f32[512]{0:T(512)S(1)}, f32[512]{0:T(512)}, u32[]{:S(2)}) copy-start(f32[512]{0:T(512)} %copy-done.37) | copy-start | bytes 6148
  1535.3 9.2 copy-start.35
  1535.3 9.2 copy-start.36
  1535.3 56.1 %copy-start.9 = (f32[512,1024]{1,0:T(8,128)S(1)}, f32[512,1024]{1,0:T(8,128)}, u32[]{:S(2)}) copy-start(f32[512,1024]{1,0:T(8,128)} %copy-done.8) | copy-start | bytes 6291460
  (32 other events, 100.7 us)
Sparse Core Ops, SparseCore 0:
  9.6 49.0 all-gather.10
  80.9 35.3 all-gather.12
  232.6 58.2 all-gather.14
  307.8 58.7 all-gather.16
  728.1 286.9 all-reduce.13
  1143.2 30.8 reduce-scatter.11
  1437.9 56.4 reduce-scatter.9
  1497.4 19.5 reduce-scatter.13
  1520.8 72.3 all-reduce.11
  1595.2 175.7 all-gather.18
